TPU v7x, 32 devices: a whole 2x2x4 slice. The times are simulated.
32 devices in a mesh: ctx: 4 (over y, core), head: 2 (over x), dp: 4 (over z).
Axes of the slice: x: 2, y: 2, z: 4, core: 2. Of those that a mesh axis runs over, the one named last changes fastest.
Arguments:
- queries: bfloat16 [1024, 6144], P(('dp', 'ctx', 'head')), parts along dimension 0, may hold values from -18 to 18
- keys: bfloat16 [1024, 1024], P(('dp', 'ctx', 'head')), parts along dimension 0, may hold values from -9 to 9
- values: bfloat16 [1024, 1024], P(('dp', 'ctx', 'head')), parts along dimension 0, may hold values from -6 to 6
- level_gain: float32 [64, 6144], P(None, 'head'), may hold values from 0.5 to 4
- levels: int32 [16], P('dp'), parts along dimension 0, may hold values from 0 to 63
- visible: int32 [16, 4], P('dp'), parts along dimension 0, may hold values from 0 to 1, as said below
- counts: int32 [16], P('dp'), parts along dimension 0, may hold values from 32 to 64, as said below
Outputs:
- mixed: bfloat16 [1024, 6144], P(('dp', 'ctx', 'head')), parts along dimension 0
- finished: bfloat16 [256, 6144], P(('dp', 'ctx'), 'head'), parts along dimension 0
There are 4 independent parts, one for each index of `dp`. A program takes and returns all parts, laid end to end along the dimension named above; an argument that names none is the same for every part. Nothing has to cross between parts.
Inputs may be any that keep to these rules, and one draw needn't show every extreme that they name: visible[c][c] is 1, visible[c][d] is 0 for d > c, and entries below the diagonal are 0 or 1. `counts`: every clip has at least half of its slots live, and in every draw some clip has all 64 live.
All inputs are finite; a program needn't handle non-finite values.
Results may differ from a plain program's by a relative error of at most 0.0045.
Values may be sent and summed in bfloat16 or wider, within the bound.
No kernel may reach another device: no remote copies, remote signals or barrier semaphores. Data moves between devices by JAX's collectives and lax.ppermute only.
A program may use at most 64 MiB of HBM per device.

v0:
```python
import math
import jax
import jax.numpy as jnp
from jax import lax
from jax.sharding import PartitionSpec as P

QUERY_HEADS = 48
KEY_VALUE_HEADS = 8
HEAD_SIZE = 128
LEVELS = 64
CLIPS = 4


def from_behind(block, axis, distance):
    devices = range(lax.axis_size(axis))
    route = [(i - distance, i) for i in devices if i - distance in devices]
    return lax.ppermute(block, axis, route)


def body(queries, keys, values, level_gain, levels, visible, counts):
    head_count = lax.axis_size("head")
    ctx_count = lax.axis_size("ctx")
    ctx_index = lax.axis_index("ctx")
    tok_rows = queries.shape[0]
    rows_ctx = tok_rows * head_count
    clip_tok = rows_ctx * ctx_count // CLIPS
    heads_per_group = QUERY_HEADS // KEY_VALUE_HEADS
    scale = 1.0 / math.sqrt(HEAD_SIZE)
    clip_range = jnp.arange(CLIPS, dtype=jnp.int32)
    source_count = ctx_count // CLIPS
    query_local, key_local, value_local = (
        lax.all_to_all(queries, "head", split_axis=1, concat_axis=0, tiled=True),
        lax.all_to_all(keys, "head", split_axis=1, concat_axis=0, tiled=True),
        lax.all_to_all(values, "head", split_axis=1, concat_axis=0, tiled=True),
    )
    query_width = query_local.shape[1]
    query_ids = ctx_index * rows_ctx + jnp.arange(rows_ctx, dtype=jnp.int32)
    row_groups = [(0, rows_ctx)]
    query_grouped = query_local.reshape(rows_ctx, -1, heads_per_group, HEAD_SIZE)
    local_kv_heads = query_grouped.shape[1]
    query_onehot = (query_ids // clip_tok)[:, None] == clip_range[None, :]
    query_count = jnp.sum(jnp.where(query_onehot, counts[None, :], 0), axis=1)
    query_live = query_ids % clip_tok < query_count
    query_sees = jnp.sum(jnp.where(query_onehot[:, :, None], visible[None, :, :], 0), axis=1) == 1
    query_level = jnp.sum(jnp.where(query_onehot, levels[None, :], 0), axis=1)

    def key_block(carry_state, key_block_rows, value_block_rows, first_row):
        block_rows = key_block_rows.shape[0]
        key_ids = first_row + jnp.arange(block_rows, dtype=jnp.int32)
        key_onehot = (key_ids // clip_tok)[:, None] == clip_range[None, :]
        key_count = jnp.sum(jnp.where(key_onehot, counts[None, :], 0), axis=1)
        key_live = key_ids % clip_tok < key_count
        block_clips = jnp.any(key_onehot & key_live[:, None], axis=0)
        key_head_rows = key_block_rows.reshape(block_rows, -1, HEAD_SIZE)
        value_head_rows = value_block_rows.reshape(block_rows, -1, HEAD_SIZE)
        group_start, group_rows = row_groups[0]
        group_end = group_start + group_rows
        part_state = tuple((member for member in carry_state))
        group_sees = query_sees
        needed = jnp.any(jnp.any(group_sees, axis=0) & block_clips)

        def update(state, group_sees=group_sees, group_start=group_start, group_end=group_end):
            running_max, denominator, weighted = state
            allowed = (
                jnp.any(group_sees[:, None, :] & key_onehot[None, :, :], axis=-1)
                & key_live[None, :]
            )
            scores = (
                jnp.einsum(
                    "rkgd,nkd->rkgn",
                    query_grouped,
                    key_head_rows,
                    preferred_element_type=jnp.float32,
                )
                * scale
            )
            key_mask = allowed[:, None, None, :]
            scores = jnp.where(key_mask, scores, -1e30)
            new_max = jnp.maximum(running_max, jnp.max(scores, axis=-1))
            weights = jnp.where(key_mask, jnp.exp(scores - new_max[..., None]), 0.0)
            shrink = jnp.exp(running_max - new_max)
            denominator = denominator * shrink + jnp.sum(weights, axis=-1)
            weighted = weighted * shrink[..., None] + jnp.einsum(
                "rkgn,nkd->rkgd",
                weights.astype(jnp.bfloat16),
                value_head_rows,
                preferred_element_type=jnp.float32,
            )
            return (new_max, denominator, weighted)

        def keep(state):
            return state

        group_states = [lax.cond(needed, update, keep, part_state)]
        if len(group_states) == 1:
            return group_states[0]
        return tuple(
            (
                jnp.concatenate([state[member] for state in group_states], axis=0)
                for member in range(3)
            )
        )

    initial = (
        jnp.full((rows_ctx, local_kv_heads, heads_per_group), -1e30, jnp.float32),
        jnp.zeros((rows_ctx, local_kv_heads, heads_per_group), jnp.float32),
        jnp.zeros((rows_ctx, local_kv_heads, heads_per_group, HEAD_SIZE), jnp.float32),
    )
    key_piece = lax.all_gather(key_local, "ctx", axis=0, tiled=True)
    value_piece = lax.all_gather(value_local, "ctx", axis=0, tiled=True)
    piece_rows = key_piece.shape[0]
    block_rows = math.gcd(piece_rows, 512)

    def advance(block_index, inner_state):
        key_slice = lax.dynamic_slice_in_dim(key_piece, block_index * block_rows, block_rows, 0)
        value_slice = lax.dynamic_slice_in_dim(value_piece, block_index * block_rows, block_rows, 0)
        return key_block(inner_state, key_slice, value_slice, block_index * block_rows)

    final_state = lax.fori_loop(0, piece_rows // block_rows, advance, initial)
    attended = (final_state[2] / final_state[1][..., None]).reshape(rows_ctx, query_width)
    level_onehot = (query_level[:, None] == jnp.arange(LEVELS, dtype=jnp.int32)[None, :]).astype(
        jnp.float32
    )
    gate_rows = jnp.dot(
        level_onehot,
        level_gain,
        precision=lax.Precision.HIGHEST,
        preferred_element_type=jnp.float32,
    )
    gated = jnp.where(query_live[:, None], attended * gate_rows, 0.0).astype(jnp.bfloat16)
    mixed = lax.all_to_all(gated, "head", split_axis=0, concat_axis=1, tiled=True)
    relay_rows = rows_ctx // CLIPS
    held = jnp.where(ctx_index < source_count, gated, jnp.zeros_like(gated)).reshape(
        CLIPS, relay_rows, query_width
    )
    empty_block = jnp.zeros_like(held)
    sources = jnp.arange(source_count, dtype=jnp.int32)
    hop_bits = (source_count - 1).bit_length()
    for bit_number in reversed(range(hop_bits)):
        higher = sources >> bit_number + 1 << bit_number + 1
        places = sources + 3 * higher
        holds_bit = jnp.any((places == ctx_index) & (sources >> bit_number & 1 == 1))
        moving = jnp.where(holds_bit, held, empty_block)
        staying = jnp.where(holds_bit, empty_block, held)
        arriving = from_behind(moving, "ctx", 3 * (1 << bit_number))
        held = staying + arriving
    group_position = ctx_index % CLIPS
    finished = held[0]
    for lane_number in range(1, CLIPS):
        arriving_tile = from_behind(held[lane_number], "ctx", lane_number)
        finished = jnp.where(group_position == lane_number, arriving_tile, finished)
    return (mixed, finished)


def solution(mesh):
    placed = (
        P(("dp", "ctx", "head"), None),
        P(("dp", "ctx", "head"), None),
        P(("dp", "ctx", "head"), None),
        P(None, "head"),
        P("dp"),
        P("dp", None),
        P("dp"),
    )
    return jax.shard_map(
        body,
        mesh=mesh,
        in_specs=placed,
        out_specs=(P(("dp", "ctx", "head"), None), P(("dp", "ctx"), "head")),
        check_vma=False,
    )
```

profile of v0, /device:TPU:0, one launch (start us, length us, event | category | flops | bytes accessed | tf_op | source)
XLA Modules:
  0.0 61.5 jit_solution(9454937511669953927)
XLA Ops:
  0.6 1.5 %copy.71 = bf16[4,2,8,512]{3,2,0,1:T(8,128)(2,1)} copy(bf16[4,2,8,512]{3,2,1,0:T(8,128)(2,1)} %bitcast.40) | data formatting | bytes 131072 | tf_op jit(solution)/shard_map/all_to_all | solution.py:33
  2.2 4.2 %all-to-all-start = ((bf16[32,2,512]{2,0,1:T(8,128)(2,1)}), bf16[32,2,512]{2,0,1:T(8,128)(2,1)S(1)}, u32[]{:S(2)}, u32[]{:S(2)}) async-start(bf16[32,2,512]{2,0,1:T(8,128)(2,1)} %bitcast.31), calls=%async_computation | async-start | bytes 131072 | tf_op jit(solution)/shard_map/all_to_all | solution.py:33
  6.5 0.8 %select_reduce_fusion = s32[64,4]{0,1:T(4,128)S(1)} fusion(s32[4,4]{1,0:T(4,128)} %param.14, pred[64,4]{0,1:T(4,128)(4,1)S(1)} %iota_compare_fusion.3), kind=kLoop, calls=%fused_computation.33 | loop fusion | flops 1792 | bytes 1344 | tf_op jit(solution)/shard_map/reduce_sum | solution.py:44
  8.2 0.8 %select_reduce_fusion.2 = (s32[64]{0:T(128)S(1)}, s32[64]{0:T(128)S(1)}) fusion(s32[4]{0:T(128)} %param.13, s32[64]{0:T(128)S(1)} %and_select_fusion.3, s32[4]{0:T(128)} %param.15), kind=kLoop, calls=%fused_computation.37 | loop fusion | flops 1152 | bytes 800 | tf_op jit(solution)/shard_map/reduce_sum | solution.py:45
  9.6 1.5 %copy.70 = bf16[4,2,8,512]{3,2,0,1:T(8,128)(2,1)} copy(bf16[4,2,8,512]{3,2,1,0:T(8,128)(2,1)} %bitcast.41) | data formatting | bytes 131072 | tf_op jit(solution)/shard_map/all_to_all | solution.py:34
  11.1 3.3 %all-to-all-start.2 = ((bf16[32,2,512]{2,0,1:T(8,128)(2,1)}), bf16[32,2,512]{2,0,1:T(8,128)(2,1)S(1)}, u32[]{:S(2)}, u32[]{:S(2)}) async-start(bf16[32,2,512]{2,0,1:T(8,128)(2,1)} %bitcast.30), calls=%async_computation.2 | async-start | bytes 131072 | tf_op jit(solution)/shard_map/all_to_all | solution.py:34
  15.1 1.8 %copy.69 = bf16[4,2,8,3072]{3,2,0,1:T(8,128)(2,1)} copy(bf16[4,2,8,3072]{3,2,1,0:T(8,128)(2,1)} %bitcast.35) | data formatting | bytes 786432 | tf_op jit(solution)/shard_map/all_to_all | solution.py:32
  16.9 1.6 %all-to-all-done.2 = bf16[32,2,512]{2,0,1:T(8,128)(2,1)S(1)} async-done(((bf16[32,2,512]{2,0,1:T(8,128)(2,1)}), bf16[32,2,512]{2,0,1:T(8,128)(2,1)S(1)}, u32[]{:S(2)}, u32[]{:S(2)}) %all-to-all-start.2) | async-done | bytes 65568 | tf_op jit(solution)/shard_map/all_to_all | solution.py:34
  18.5 3.5 %all-to-all-start.1 = ((bf16[32,2,3072]{2,0,1:T(8,128)(2,1)}), bf16[32,2,3072]{2,0,1:T(8,128)(2,1)S(1)}, u32[]{:S(2)}, u32[]{:S(2)}) async-start(bf16[32,2,3072]{2,0,1:T(8,128)(2,1)} %bitcast.29), calls=%async_computation.1 | async-start | bytes 786432 | tf_op jit(solution)/shard_map/all_to_all | solution.py:32
  22.0 6.3 %all_gather.6 = bf16[256,512]{1,0:T(8,128)(2,1)S(1)} all-gather(bf16[64,512]{1,0:T(8,128)(2,1)S(1)} %bitcast.37), channel_id=1, replica_groups=mesh['ctx'=4,'head'=2,'dp'=4] {'ctx'}, dimensions={0}, use_global_device_ids=true | all-gather | bytes 327680 | tf_op jit(solution)/shard_map/all_gather | solution.py:109
  28.3 5.8 %all_gather.7 = bf16[256,512]{1,0:T(8,128)(2,1)S(1)} all-gather(bf16[64,512]{1,0:T(8,128)(2,1)S(1)} %bitcast.38), channel_id=1, replica_groups=mesh['ctx'=4,'head'=2,'dp'=4] {'ctx'}, dimensions={0}, use_global_device_ids=true | all-gather | bytes 327680 | tf_op jit(solution)/shard_map/all_gather | solution.py:110
  34.2 6.7 %conditional.1 = ((f32[64,4,6]{0,2,1:T(8,128)S(1)}, f32[64,4,6,128]{3,0,2,1:T(8,128)S(1)})) conditional(s32[]{:T(128)} %convert_element_type.13, (f32[64,4,6]{0,2,1:T(8,128)S(1)}, f32[64,4,6,128]{3,0,2,1:T(8,128)S(1)}) %tuple.31, (pred[64,4]{0,1:T(4,128)(4,1)S(1)}, pred[256,4]{0,1:T(4,128)(4,1)S(1)}, s32[256]{0:T(256)S(1)}, s32[256]{0:T(256)S(1)}, ...), branch_computations={%region_6.7_spmd, %region_7.11_spmd} | conditional | flops 205395968 | bytes 9220888 | solution.py:94
  34.2 1.3 %reshape.148 = bf16[64,4,6,128]{3,2,1,0:T(8,128)(2,1)} reshape(bf16[2,32,3072]{2,1,0:T(8,128)(2,1)S(1)} %get-tuple-element.127) | data formatting | bytes 786432 | tf_op jit(solution)/shard_map/reshape | solution.py:39
  35.4 0.8 %reshape.147 = bf16[256,4,128]{2,1,0:T(4,128)(2,1)} reshape(bf16[256,512]{1,0:T(8,128)(2,1)S(1)} %get-tuple-element.126) | data formatting | bytes 524288 | tf_op jit(solution)/shard_map/while/body/eval_jaxpr/reshape | solution.py:54
  36.4 1.6 %fusion.21 = (f32[64,4,6]{0,2,1:T(8,128)S(1)}, f32[64,4,6,256]{3,0,2,1:T(8,128)S(1)}) fusion(bf16[64,4,6,128]{3,2,1,0:T(8,128)(2,1)} %reshape.148, bf16[256,4,128,1]{2,1,0,3:T(4,128)(2,1)} %bitcast.39, pred[64,256]{1,0:T(8,128)(4,1)S(1)} %broadcast_and_fusion), kind=kOutput, calls=%fused_computation.57 | convolution fusion | flops 101841408 | bytes 2250752 | tf_op jit(solution)/shard_map/while/body/eval_jaxpr/cond/branch_1_fun/rkgd,nkd->rkgn/dot_general | solution.py:69
  38.6 0.8 %reshape.149 = bf16[256,4,128]{2,1,0:T(4,128)(2,1)} reshape(bf16[256,512]{1,0:T(8,128)(2,1)S(1)} %get-tuple-element.129) | data formatting | bytes 524288 | tf_op jit(solution)/shard_map/while/body/eval_jaxpr/reshape | solution.py:55
  39.3 1.6 %fusion = f32[64,4,6,128]{3,0,2,1:T(8,128)S(1)} fusion(f32[64,4,6,256]{3,0,2,1:T(8,128)S(1)} %get-tuple-element.153, f32[64,4,6,128]{3,0,2,1:T(8,128)S(1)} %get-tuple-element.128, f32[64,4,6]{0,2,1:T(8,128)S(1)} %broadcast_maximum_fusion, pred[64,256]{1,0:T(8,128)(4,1)S(1)} %broadcast_and_fusion, f32[64,4,6]{0,2,1:T(8,128)S(1)} %get-tuple-element.150, ...), kind=kOutput, calls=%fused_computation.3 | convolution fusion | flops 102236160 | bytes 3436544 | tf_op jit(solution)/shard_map/while/body/eval_jaxpr/cond/branch_1_fun/rkgn,nkd->rkgd/dot_general | solution.py:83
  41.9 1.3 %broadcast_select_fusion = (bf16[64,3072]{1,0:T(8,128)(2,1)S(1)}, bf16[64,3072]{1,0:T(8,128)(2,1)}) fusion(pred[]{:T(512)S(6)} %lt.53, f32[64,3072]{1,0:T(8,128)S(1)} %reshape.151, f32[64,3072]{1,0:T(8,128)S(1)} %copy-done, s32[64]{0:T(128)S(1)} %get-tuple-element.146, pred[64]{0:T(512)(128)(4,1)S(1)} %fusion.19), kind=kOutput, calls=%fused_computation.25 | convolution fusion | flops 151785472 | bytes 2359617 | tf_op jit(solution)/shard_map/dot_general | solution.py:124
  43.2 3.4 %collective-permute-start = (bf16[16,3072]{1,0:T(8,128)(2,1)S(1)}, bf16[16,3072]{1,0:T(8,128)(2,1)S(1)}, u32[]{:S(2)}, u32[]{:S(2)}) collective-permute-start(bf16[16,3072]{1,0:T(8,128)(2,1)S(1)} %get-tuple-element.156), channel_id=1, source_target_pairs={{0,24},{1,25},{2,26},{3,27},{4,28},{5,29},{6,30},{7,31}} | collective-permute-start | bytes 294920 | tf_op jit(solution)/shard_map/ppermute | solution.py:17
  46.6 1.3 %collective-permute-start.1 = (bf16[16,3072]{1,0:T(8,128)(2,1)S(1)}, bf16[16,3072]{1,0:T(8,128)(2,1)S(1)}, u32[]{:S(2)}, u32[]{:S(2)}) collective-permute-start(bf16[16,3072]{1,0:T(8,128)(2,1)S(1)} %get-tuple-element.155), channel_id=1, source_target_pairs={{0,16},{8,24},{1,17},{9,25},{2,18},{10,26},{3,19},{11,27},{4,20},{... | collective-permute-start | bytes 294920 | tf_op jit(solution)/shard_map/ppermute | solution.py:17
  47.9 2.0 %collective-permute-start.2 = (bf16[16,3072]{1,0:T(8,128)(2,1)S(1)}, bf16[16,3072]{1,0:T(8,128)(2,1)S(1)}, u32[]{:S(2)}, u32[]{:S(2)}) collective-permute-start(bf16[16,3072]{1,0:T(8,128)(2,1)S(1)} %get-tuple-element.154), channel_id=1, source_target_pairs={{0,8},{8,16},{16,24},{1,9},{9,17},{17,25},{2,10},{10,18},{18,26},{... | collective-permute-start | bytes 294920 | tf_op jit(solution)/shard_map/ppermute | solution.py:17
  50.0 3.5 %all-to-all-start.3 = ((bf16[2,32,3072]{2,1,0:T(8,128)(2,1)}), bf16[2,32,3072]{2,1,0:T(8,128)(2,1)S(1)}, u32[]{:S(2)}, u32[]{:S(2)}) async-start(bf16[2,32,3072]{2,1,0:T(8,128)(2,1)} %bitcast.9), calls=%async_computation.3 | async-start | bytes 786432 | tf_op jit(solution)/shard_map/all_to_all | solution.py:131
  54.1 6.6 %all-to-all-done.3 = bf16[2,32,3072]{2,1,0:T(8,128)(2,1)S(1)} async-done(((bf16[2,32,3072]{2,1,0:T(8,128)(2,1)}), bf16[2,32,3072]{2,1,0:T(8,128)(2,1)S(1)}, u32[]{:S(2)}, u32[]{:S(2)}) %all-to-all-start.3) | async-done | bytes 393248 | tf_op jit(solution)/shard_map/all_to_all | solution.py:131
  60.7 0.8 %copy.55 = bf16[2,4,8,3072]{3,2,0,1:T(8,128)(2,1)} copy(bf16[2,4,8,3072]{3,2,1,0:T(8,128)(2,1)S(1)} %bitcast.33) | data formatting | bytes 786432 | tf_op jit(solution)/shard_map/all_to_all | solution.py:131
  (31 shorter events, 4.1 us)
Async XLA Ops:
  0.6 41.2 %copy-start = (f32[64,3072]{1,0:T(8,128)S(1)}, f32[64,3072]{1,0:T(8,128)}, u32[]{:S(2)}) copy-start(f32[64,3072]{1,0:T(8,128)} %param.12) | copy-start | bytes 2359300
  2.2 8.9 %all-to-all-start = ((bf16[32,2,512]{2,0,1:T(8,128)(2,1)}), bf16[32,2,512]{2,0,1:T(8,128)(2,1)S(1)}, u32[]{:S(2)}, u32[]{:S(2)}) async-start(bf16[32,2,512]{2,0,1:T(8,128)(2,1)} %bitcast.31), calls=%async_computation | async-start | bytes 131072 | tf_op jit(solution)/shard_map/all_to_all | solution.py:33
  11.1 7.4 %all-to-all-start.2 = ((bf16[32,2,512]{2,0,1:T(8,128)(2,1)}), bf16[32,2,512]{2,0,1:T(8,128)(2,1)S(1)}, u32[]{:S(2)}, u32[]{:S(2)}) async-start(bf16[32,2,512]{2,0,1:T(8,128)(2,1)} %bitcast.30), calls=%async_computation.2 | async-start | bytes 131072 | tf_op jit(solution)/shard_map/all_to_all | solution.py:34
  18.5 15.6 %all-to-all-start.1 = ((bf16[32,2,3072]{2,0,1:T(8,128)(2,1)}), bf16[32,2,3072]{2,0,1:T(8,128)(2,1)S(1)}, u32[]{:S(2)}, u32[]{:S(2)}) async-start(bf16[32,2,3072]{2,0,1:T(8,128)(2,1)} %bitcast.29), calls=%async_computation.1 | async-start | bytes 786432 | tf_op jit(solution)/shard_map/all_to_all | solution.py:32
  43.2 10.2 %collective-permute-start = (bf16[16,3072]{1,0:T(8,128)(2,1)S(1)}, bf16[16,3072]{1,0:T(8,128)(2,1)S(1)}, u32[]{:S(2)}, u32[]{:S(2)}) collective-permute-start(bf16[16,3072]{1,0:T(8,128)(2,1)S(1)} %get-tuple-element.156), channel_id=1, source_target_pairs={{0,24},{1,25},{2,26},{3,27},{4,28},{5,29},{6,30},{7,31}} | collective-permute-start | bytes 294920 | tf_op jit(solution)/shard_map/ppermute | solution.py:17
  46.6 6.8 %collective-permute-start.1 = (bf16[16,3072]{1,0:T(8,128)(2,1)S(1)}, bf16[16,3072]{1,0:T(8,128)(2,1)S(1)}, u32[]{:S(2)}, u32[]{:S(2)}) collective-permute-start(bf16[16,3072]{1,0:T(8,128)(2,1)S(1)} %get-tuple-element.155), channel_id=1, source_target_pairs={{0,16},{8,24},{1,17},{9,25},{2,18},{10,26},{3,19},{11,27},{4,20},{... | collective-permute-start | bytes 294920 | tf_op jit(solution)/shard_map/ppermute | solution.py:17
  47.9 5.6 %collective-permute-start.2 = (bf16[16,3072]{1,0:T(8,128)(2,1)S(1)}, bf16[16,3072]{1,0:T(8,128)(2,1)S(1)}, u32[]{:S(2)}, u32[]{:S(2)}) collective-permute-start(bf16[16,3072]{1,0:T(8,128)(2,1)S(1)} %get-tuple-element.154), channel_id=1, source_target_pairs={{0,8},{8,16},{16,24},{1,9},{9,17},{17,25},{2,10},{10,18},{18,26},{... | collective-permute-start | bytes 294920 | tf_op jit(solution)/shard_map/ppermute | solution.py:17
  50.0 10.7 %all-to-all-start.3 = ((bf16[2,32,3072]{2,1,0:T(8,128)(2,1)}), bf16[2,32,3072]{2,1,0:T(8,128)(2,1)S(1)}, u32[]{:S(2)}, u32[]{:S(2)}) async-start(bf16[2,32,3072]{2,1,0:T(8,128)(2,1)} %bitcast.9), calls=%async_computation.3 | async-start | bytes 786432 | tf_op jit(solution)/shard_map/all_to_all | solution.py:131
where the time goes:
time: 62.2 us; the launch traced here: 61.5 us
  starting transfers between devices  21.2 us (34%)
  blocking collectives  12.1 us (19%)
  local copies, waits for them, and re-layouts  9.12 us (15%)
  waiting for transfers between devices  8.19 us (13%)
  other arithmetic  4.82 us (8%)
  matrix products  4.5 us (7%)
  between operations  1.43 us (2%)
    ppermute x3, starting transfers between devices, from_behind(): return lax.ppermute(block, axis, route)  6.7 us
    all_to_all x1, waiting for transfers between devices, body(): lax.all_to_all(gated, 'head', split_axis=0, concat_axis=1, tiled=True)  6.56 us
    all_gather x1, blocking collectives, body(): key_piece = lax.all_gather(key_local, 'ctx', axis=0, tiled=True)  6.31 us
    all_gather x1, blocking collectives, body(): value_piece = lax.all_gather(value_local, 'ctx', axis=0, tiled=True)  5.84 us
    all_to_all x1, starting transfers between devices, body(): lax.all_to_all(keys, 'head', split_axis=1, concat_axis=0, tiled=True)  4.23 us
    all_to_all x1, starting transfers between devices, body(): lax.all_to_all(gated, 'head', split_axis=0, concat_axis=1, tiled=True)  3.48 us
    all_to_all x1, starting transfers between devices, body(): lax.all_to_all(queries, 'head', split_axis=1, concat_axis=0, tiled=True)  3.47 us
    all_to_all x1, starting transfers between devices, body(): lax.all_to_all(values, 'head', split_axis=1, concat_axis=0, tiled=True)  3.32 us
  transfers between devices with their start and end apart: 7, of which 2 were waited for; matrix products, arithmetic and copies ran while one was open for 12% of the time, Pallas kernels for 0%

commit v1 on v0

--- a/solution.py
+++ b/solution.py
@@ -107,7 +107,14 @@
         jnp.zeros((rows_ctx, local_kv_heads, heads_per_group, HEAD_SIZE), jnp.float32),
     )
     key_piece = lax.all_gather(key_local, "ctx", axis=0, tiled=True)
-    value_piece = lax.all_gather(value_local, "ctx", axis=0, tiled=True)
+    ways, here, step = (lax.axis_size("ctx"), lax.axis_index("ctx"), value_local.shape[0])
+    line, have = (value_local, 1)
+    while have < ways:
+        line = jnp.concatenate(
+            [line, lax.ppermute(line, "ctx", [(d, (d - have) % ways) for d in range(ways)])], axis=0
+        )
+        have = 2 * have
+    value_piece = jnp.roll(line, here * step, axis=0)
     piece_rows = key_piece.shape[0]
     block_rows = math.gcd(piece_rows, 512)
 

time: 62.2 us -> 55 us (0.88)
  blocking collectives: 12.1 us -> 6.47 us
  matrix products: 4.5 us -> 2.49 us
  local copies, waits for them, and re-layouts: 9.12 us -> 7.27 us
  starting transfers between devices: 21.2 us -> 22.6 us
  waiting for transfers between devices: 8.19 us -> 9.23 us
    all_gather x1 -> x0, blocking collectives: 5.84 us -> none  [body(): value_piece = lax.all_gather(value_local, 'ctx', axis=0, tiled=True)]
    ppermute x0 -> x2, starting transfers between devices: none -> 2.19 us  [body(): lax.ppermute(line, 'ctx', [(d, (d - have) % ways) for d in range(ways)])]
    ppermute x0 -> x2, waiting for transfers between devices: none -> 1.9 us  [body(): lax.ppermute(line, 'ctx', [(d, (d - have) % ways) for d in range(ways)])]
    all_to_all x1, waiting for transfers between devices: 1.61 us -> 0.01 us  [body(): lax.all_to_all(values, 'head', split_axis=1, concat_axis=0, tiled=True)]
    dot_general x1, matrix products: 1.63 us -> 0.49 us  [update(): jnp.einsum('rkgd,nkd->rkgn', query_grouped, key_head_rows, preferred_elem...]
    all_to_all x1, starting transfers between devices: 3.32 us -> 4.23 us  [body(): lax.all_to_all(values, 'head', split_axis=1, concat_axis=0, tiled=True)]
    all_to_all x1, starting transfers between devices: 4.23 us -> 3.33 us  [body(): lax.all_to_all(keys, 'head', split_axis=1, concat_axis=0, tiled=True)]
    dot_general x1, matrix products: 1.56 us -> 0.69 us  [update(): jnp.einsum('rkgn,nkd->rkgd', weights.astype(jnp.bfloat16), value_head_row...]
  transfers between devices with their start and end apart: 7 -> 9, of which waited for: 2 -> 3; matrix products, arithmetic and copies ran while one was open for 12% -> 13% of each run, Pallas kernels for 0% -> 0%
where the time goes in v1:
time: 55 us; the launch traced here: 54.4 us
  starting transfers between devices  22.6 us (41%)
  waiting for transfers between devices  9.23 us (17%)
  local copies, waits for them, and re-layouts  7.27 us (13%)
  blocking collectives  6.47 us (12%)
  other arithmetic  4.84 us (9%)
  matrix products  2.49 us (5%)
  between operations  1.41 us (3%)
    all_to_all x1, waiting for transfers between devices, body(): lax.all_to_all(gated, 'head', split_axis=0, concat_axis=1, tiled=True)  6.54 us
    all_gather x1, blocking collectives, body(): key_piece = lax.all_gather(key_local, 'ctx', axis=0, tiled=True)  6.47 us
    ppermute x3, starting transfers between devices, from_behind(): return lax.ppermute(block, axis, route)  5.89 us
    all_to_all x1, starting transfers between devices, body(): lax.all_to_all(values, 'head', split_axis=1, concat_axis=0, tiled=True)  4.23 us
    all_to_all x1, starting transfers between devices, body(): lax.all_to_all(gated, 'head', split_axis=0, concat_axis=1, tiled=True)  3.48 us
    all_to_all x1, starting transfers between devices, body(): lax.all_to_all(queries, 'head', split_axis=1, concat_axis=0, tiled=True)  3.47 us
    all_to_all x1, starting transfers between devices, body(): lax.all_to_all(keys, 'head', split_axis=1, concat_axis=0, tiled=True)  3.33 us
    ppermute x2, starting transfers between devices, body(): lax.ppermute(line, 'ctx', [(d, (d - have) % ways) for d in range(ways)])  2.19 us
  transfers between devices with their start and end apart: 9, of which 3 were waited for; matrix products, arithmetic and copies ran while one was open for 13% of the time, Pallas kernels for 0%

profile of v1, /device:TPU:0, one launch (start us, length us, event | category | flops | bytes accessed | tf_op | source)
XLA Modules:
  0.0 54.4 jit_solution(9873054976987318285)
XLA Ops:
  0.6 1.5 %copy.90 = bf16[4,2,8,512]{3,2,0,1:T(8,128)(2,1)} copy(bf16[4,2,8,512]{3,2,1,0:T(8,128)(2,1)} %bitcast.48) | data formatting | bytes 131072 | tf_op jit(solution)/shard_map/all_to_all | solution.py:34
  2.2 4.2 %all-to-all-start.2 = ((bf16[32,2,512]{2,0,1:T(8,128)(2,1)}), bf16[32,2,512]{2,0,1:T(8,128)(2,1)S(1)}, u32[]{:S(2)}, u32[]{:S(2)}) async-start(bf16[32,2,512]{2,0,1:T(8,128)(2,1)} %bitcast.35), calls=%async_computation.2 | async-start | bytes 131072 | tf_op jit(solution)/shard_map/all_to_all | solution.py:34
  6.4 0.8 %select_reduce_fusion = s32[64,4]{0,1:T(4,128)S(1)} fusion(s32[4,4]{1,0:T(4,128)} %param.14, pred[64,4]{0,1:T(4,128)(4,1)S(1)} %iota_compare_fusion.3), kind=kLoop, calls=%fused_computation.40 | loop fusion | flops 1792 | bytes 1344 | tf_op jit(solution)/shard_map/reduce_sum | solution.py:44
  7.3 0.7 %select_reduce_fusion.1 = s32[256]{0:T(256)S(1)} fusion(s32[4]{0:T(128)} %param.15, s32[256]{0:T(256)S(1)} %and_select_fusion.2), kind=kLoop, calls=%fused_computation.41 | loop fusion | flops 2816 | bytes 2064 | tf_op jit(solution)/shard_map/while/body/eval_jaxpr/reduce_sum | solution.py:51
  8.2 0.8 %select_reduce_fusion.2 = (s32[64]{0:T(128)S(1)}, s32[64]{0:T(128)S(1)}) fusion(s32[4]{0:T(128)} %param.13, s32[64]{0:T(128)S(1)} %and_select_fusion.3, s32[4]{0:T(128)} %param.15), kind=kLoop, calls=%fused_computation.44 | loop fusion | flops 1152 | bytes 800 | tf_op jit(solution)/shard_map/reduce_sum | solution.py:45
  9.6 1.8 %copy.89 = bf16[4,2,8,3072]{3,2,0,1:T(8,128)(2,1)} copy(bf16[4,2,8,3072]{3,2,1,0:T(8,128)(2,1)} %bitcast.44) | data formatting | bytes 786432 | tf_op jit(solution)/shard_map/all_to_all | solution.py:32
  11.4 1.5 %copy.91 = bf16[4,2,8,512]{3,2,0,1:T(8,128)(2,1)} copy(bf16[4,2,8,512]{3,2,1,0:T(8,128)(2,1)} %bitcast.49) | data formatting | bytes 131072 | tf_op jit(solution)/shard_map/all_to_all | solution.py:33
  13.5 3.3 %all-to-all-start = ((bf16[32,2,512]{2,0,1:T(8,128)(2,1)}), bf16[32,2,512]{2,0,1:T(8,128)(2,1)S(1)}, u32[]{:S(2)}, u32[]{:S(2)}) async-start(bf16[32,2,512]{2,0,1:T(8,128)(2,1)} %bitcast.36), calls=%async_computation | async-start | bytes 131072 | tf_op jit(solution)/shard_map/all_to_all | solution.py:33
  16.9 1.6 %collective-permute-start = (bf16[64,512]{1,0:T(8,128)(2,1)S(1)}, bf16[64,512]{1,0:T(8,128)(2,1)S(1)}, u32[]{:S(2)}, u32[]{:S(2)}) collective-permute-start(bf16[64,512]{1,0:T(8,128)(2,1)S(1)} %bitcast.39), channel_id=1, source_target_pairs={{0,24},{8,0},{16,8},{24,16},{1,25},{9,1},{17,9},{25,17},{2,26},{10... | collective-permute-start | bytes 196616 | tf_op jit(solution)/shard_map/ppermute | solution.py:114
  18.4 1.9 %collective-permute-done = bf16[64,512]{1,0:T(8,128)(2,1)S(1)} collective-permute-done((bf16[64,512]{1,0:T(8,128)(2,1)S(1)}, bf16[64,512]{1,0:T(8,128)(2,1)S(1)}, u32[]{:S(2)}, u32[]{:S(2)}) %collective-permute-start) | collective-permute-done | bytes 65568 | tf_op jit(solution)/shard_map/ppermute | solution.py:114
  20.3 0.6 %collective-permute-start.1 = (bf16[128,512]{1,0:T(8,128)(2,1)S(1)}, bf16[128,512]{1,0:T(8,128)(2,1)S(1)}, u32[]{:S(2)}, u32[]{:S(2)}) collective-permute-start(bf16[128,512]{1,0:T(8,128)(2,1)S(1)} %pad_maximum_fusion), channel_id=1, source_target_pairs={{0,16},{8,24},{16,0},{24,8},{1,17},{9,25},{17,1},{25,9},{2,18},{10... | collective-permute-start | bytes 393224 | tf_op jit(solution)/shard_map/ppermute | solution.py:114
  21.0 3.5 %all-to-all-start.1 = ((bf16[32,2,3072]{2,0,1:T(8,128)(2,1)}), bf16[32,2,3072]{2,0,1:T(8,128)(2,1)S(1)}, u32[]{:S(2)}, u32[]{:S(2)}) async-start(bf16[32,2,3072]{2,0,1:T(8,128)(2,1)} %bitcast.34), calls=%async_computation.1 | async-start | bytes 786432 | tf_op jit(solution)/shard_map/all_to_all | solution.py:32
  24.5 6.5 %all_gather.3 = bf16[256,512]{1,0:T(8,128)(2,1)S(1)} all-gather(bf16[64,512]{1,0:T(8,128)(2,1)S(1)} %bitcast.46), channel_id=1, replica_groups=mesh['ctx'=4,'head'=2,'dp'=4] {'ctx'}, dimensions={0}, use_global_device_ids=true | all-gather | bytes 327680 | tf_op jit(solution)/shard_map/all_gather | solution.py:109
  31.0 0.8 %all-to-all-done.1 = bf16[32,2,3072]{2,0,1:T(8,128)(2,1)S(1)} async-done(((bf16[32,2,3072]{2,0,1:T(8,128)(2,1)}), bf16[32,2,3072]{2,0,1:T(8,128)(2,1)S(1)}, u32[]{:S(2)}, u32[]{:S(2)}) %all-to-all-start.1) | async-done | bytes 393248 | tf_op jit(solution)/shard_map/all_to_all | solution.py:32
  31.8 2.9 %conditional.1 = ((f32[64,4,6]{0,2,1:T(8,128)S(1)}, f32[64,4,6,128]{3,0,2,1:T(8,128)S(1)})) conditional(s32[]{:T(128)} %convert_element_type.15, (f32[64,4,6]{0,2,1:T(8,128)S(1)}, f32[64,4,6,128]{3,0,2,1:T(8,128)S(1)}) %tuple.43, (pred[64,4]{0,1:T(4,128)(4,1)S(1)}, pred[256,4]{0,1:T(4,128)(4,1)S(1)}, s32[256]{0:T(256)S(1)}, s32[256]{0:T(256)S(1)}, ...), branch_computations={%region_6.7_spmd, %region_7.11_spmd.clone} | conditional | flops 205395968 | bytes 10270647 | solution.py:94
  34.0 0.7 %fusion = f32[64,4,6,128]{3,0,2,1:T(8,128)S(1)} fusion(bf16[256,4,128,1]{0,2,3,1:T(8,128)(2,1)S(1)} %bitcast.43, f32[64,4,6,256]{3,0,2,1:T(8,128)S(1)} %get-tuple-element.377, f32[64,4,6,128]{3,0,2,1:T(8,128)S(1)} %get-tuple-element.272, f32[64,4,6]{0,2,1:T(8,128)S(1)} %broadcast_maximum_fusion, pred[64,256]{1,0:T(8,128)(4,1)S(1)} %broadcast_and_fusion, ...), kind=kOutput, calls=%fused_computation.3 | convolution fusion | flops 102236160 | bytes 3436544 | tf_op jit(solution)/shard_map/while/body/eval_jaxpr/cond/branch_1_fun/rkgn,nkd->rkgd/dot_general | solution.py:83
  35.6 1.3 %broadcast_select_fusion = (bf16[64,3072]{1,0:T(8,128)(2,1)S(1)}, bf16[64,3072]{1,0:T(8,128)(2,1)}) fusion(pred[]{:T(512)S(6)} %lt.71, f32[64,3072]{1,0:T(8,128)S(1)} %reshape.157, f32[64,3072]{1,0:T(8,128)S(1)} %copy-done, s32[64]{0:T(128)S(1)} %get-tuple-element.370, pred[64]{0:T(512)(128)(4,1)S(1)} %fusion.18), kind=kOutput, calls=%fused_computation.25 | convolution fusion | flops 151785472 | bytes 2359617 | tf_op jit(solution)/shard_map/dot_general | solution.py:131
  37.0 2.6 %collective-permute-start.2 = (bf16[16,3072]{1,0:T(8,128)(2,1)S(1)}, bf16[16,3072]{1,0:T(8,128)(2,1)S(1)}, u32[]{:S(2)}, u32[]{:S(2)}) collective-permute-start(bf16[16,3072]{1,0:T(8,128)(2,1)S(1)} %get-tuple-element.380), channel_id=1, source_target_pairs={{0,24},{1,25},{2,26},{3,27},{4,28},{5,29},{6,30},{7,31}} | collective-permute-start | bytes 294920 | tf_op jit(solution)/shard_map/ppermute | solution.py:17
  39.5 1.8 %collective-permute-start.3 = (bf16[16,3072]{1,0:T(8,128)(2,1)S(1)}, bf16[16,3072]{1,0:T(8,128)(2,1)S(1)}, u32[]{:S(2)}, u32[]{:S(2)}) collective-permute-start(bf16[16,3072]{1,0:T(8,128)(2,1)S(1)} %get-tuple-element.379), channel_id=1, source_target_pairs={{0,16},{8,24},{1,17},{9,25},{2,18},{10,26},{3,19},{11,27},{4,20},{... | collective-permute-start | bytes 294920 | tf_op jit(solution)/shard_map/ppermute | solution.py:17
  41.4 1.5 %collective-permute-start.4 = (bf16[16,3072]{1,0:T(8,128)(2,1)S(1)}, bf16[16,3072]{1,0:T(8,128)(2,1)S(1)}, u32[]{:S(2)}, u32[]{:S(2)}) collective-permute-start(bf16[16,3072]{1,0:T(8,128)(2,1)S(1)} %get-tuple-element.378), channel_id=1, source_target_pairs={{0,8},{8,16},{16,24},{1,9},{9,17},{17,25},{2,10},{10,18},{18,26},{... | collective-permute-start | bytes 294920 | tf_op jit(solution)/shard_map/ppermute | solution.py:17
  42.9 3.5 %all-to-all-start.3 = ((bf16[2,32,3072]{2,1,0:T(8,128)(2,1)}), bf16[2,32,3072]{2,1,0:T(8,128)(2,1)S(1)}, u32[]{:S(2)}, u32[]{:S(2)}) async-start(bf16[2,32,3072]{2,1,0:T(8,128)(2,1)} %bitcast.6), calls=%async_computation.3 | async-start | bytes 786432 | tf_op jit(solution)/shard_map/all_to_all | solution.py:138
  46.4 0.7 %fusion.14 = bf16[16,3072]{1,0:T(8,128)(2,1)} fusion(bf16[16,3072]{1,0:T(8,128)(2,1)S(1)} %collective-permute-done.2, bf16[16,3072]{1,0:T(8,128)(2,1)S(1)} %collective-permute-done.3, bf16[16,3072]{1,0:T(8,128)(2,1)S(1)} %collective-permute-done.4, bf16[64,3072]{1,0:T(8,128)(2,1)S(1)} %get-tuple-element.383, pred[]{:T(512)S(6)} %eq.100, pred[]{:T(512)S(6)} %eq.99, ...), kind=kLoop, calls=%fused_computation.29 | loop fusion | flops 147456 | bytes 491523 | tf_op jit(solution)/shard_map/jit(_where)/select_n | solution.py:158
  47.1 6.5 %all-to-all-done.3 = bf16[2,32,3072]{2,1,0:T(8,128)(2,1)S(1)} async-done(((bf16[2,32,3072]{2,1,0:T(8,128)(2,1)}), bf16[2,32,3072]{2,1,0:T(8,128)(2,1)S(1)}, u32[]{:S(2)}, u32[]{:S(2)}) %all-to-all-start.3) | async-done | bytes 393248 | tf_op jit(solution)/shard_map/all_to_all | solution.py:138
  53.6 0.8 %copy.77 = bf16[2,4,8,3072]{3,2,0,1:T(8,128)(2,1)} copy(bf16[2,4,8,3072]{3,2,1,0:T(8,128)(2,1)S(1)} %bitcast.38) | data formatting | bytes 786432 | tf_op jit(solution)/shard_map/all_to_all | solution.py:138
  (43 shorter events, 4.2 us)
Async XLA Ops:
  0.6 35.0 %copy-start = (f32[64,3072]{1,0:T(8,128)S(1)}, f32[64,3072]{1,0:T(8,128)}, u32[]{:S(2)}) copy-start(f32[64,3072]{1,0:T(8,128)} %param.12) | copy-start | bytes 2359300
  2.2 11.3 %all-to-all-start.2 = ((bf16[32,2,512]{2,0,1:T(8,128)(2,1)}), bf16[32,2,512]{2,0,1:T(8,128)(2,1)S(1)}, u32[]{:S(2)}, u32[]{:S(2)}) async-start(bf16[32,2,512]{2,0,1:T(8,128)(2,1)} %bitcast.35), calls=%async_computation.2 | async-start | bytes 131072 | tf_op jit(solution)/shard_map/all_to_all | solution.py:34
  13.5 7.5 %all-to-all-start = ((bf16[32,2,512]{2,0,1:T(8,128)(2,1)}), bf16[32,2,512]{2,0,1:T(8,128)(2,1)S(1)}, u32[]{:S(2)}, u32[]{:S(2)}) async-start(bf16[32,2,512]{2,0,1:T(8,128)(2,1)} %bitcast.36), calls=%async_computation | async-start | bytes 131072 | tf_op jit(solution)/shard_map/all_to_all | solution.py:33
  16.9 3.5 %collective-permute-start = (bf16[64,512]{1,0:T(8,128)(2,1)S(1)}, bf16[64,512]{1,0:T(8,128)(2,1)S(1)}, u32[]{:S(2)}, u32[]{:S(2)}) collective-permute-start(bf16[64,512]{1,0:T(8,128)(2,1)S(1)} %bitcast.39), channel_id=1, source_target_pairs={{0,24},{8,0},{16,8},{24,16},{1,25},{9,1},{17,9},{25,17},{2,26},{10... | collective-permute-start | bytes 196616 | tf_op jit(solution)/shard_map/ppermute | solution.py:114
  20.3 10.6 %collective-permute-start.1 = (bf16[128,512]{1,0:T(8,128)(2,1)S(1)}, bf16[128,512]{1,0:T(8,128)(2,1)S(1)}, u32[]{:S(2)}, u32[]{:S(2)}) collective-permute-start(bf16[128,512]{1,0:T(8,128)(2,1)S(1)} %pad_maximum_fusion), channel_id=1, source_target_pairs={{0,16},{8,24},{16,0},{24,8},{1,17},{9,25},{17,1},{25,9},{2,18},{10... | collective-permute-start | bytes 393224 | tf_op jit(solution)/shard_map/ppermute | solution.py:114
  21.0 10.8 %all-to-all-start.1 = ((bf16[32,2,3072]{2,0,1:T(8,128)(2,1)}), bf16[32,2,3072]{2,0,1:T(8,128)(2,1)S(1)}, u32[]{:S(2)}, u32[]{:S(2)}) async-start(bf16[32,2,3072]{2,0,1:T(8,128)(2,1)} %bitcast.34), calls=%async_computation.1 | async-start | bytes 786432 | tf_op jit(solution)/shard_map/all_to_all | solution.py:32
  37.0 9.4 %collective-permute-start.2 = (bf16[16,3072]{1,0:T(8,128)(2,1)S(1)}, bf16[16,3072]{1,0:T(8,128)(2,1)S(1)}, u32[]{:S(2)}, u32[]{:S(2)}) collective-permute-start(bf16[16,3072]{1,0:T(8,128)(2,1)S(1)} %get-tuple-element.380), channel_id=1, source_target_pairs={{0,24},{1,25},{2,26},{3,27},{4,28},{5,29},{6,30},{7,31}} | collective-permute-start | bytes 294920 | tf_op jit(solution)/shard_map/ppermute | solution.py:17
  39.5 6.8 %collective-permute-start.3 = (bf16[16,3072]{1,0:T(8,128)(2,1)S(1)}, bf16[16,3072]{1,0:T(8,128)(2,1)S(1)}, u32[]{:S(2)}, u32[]{:S(2)}) collective-permute-start(bf16[16,3072]{1,0:T(8,128)(2,1)S(1)} %get-tuple-element.379), channel_id=1, source_target_pairs={{0,16},{8,24},{1,17},{9,25},{2,18},{10,26},{3,19},{11,27},{4,20},{... | collective-permute-start | bytes 294920 | tf_op jit(solution)/shard_map/ppermute | solution.py:17
  41.4 5.0 %collective-permute-start.4 = (bf16[16,3072]{1,0:T(8,128)(2,1)S(1)}, bf16[16,3072]{1,0:T(8,128)(2,1)S(1)}, u32[]{:S(2)}, u32[]{:S(2)}) collective-permute-start(bf16[16,3072]{1,0:T(8,128)(2,1)S(1)} %get-tuple-element.378), channel_id=1, source_target_pairs={{0,8},{8,16},{16,24},{1,9},{9,17},{17,25},{2,10},{10,18},{18,26},{... | collective-permute-start | bytes 294920 | tf_op jit(solution)/shard_map/ppermute | solution.py:17
  42.9 10.7 %all-to-all-start.3 = ((bf16[2,32,3072]{2,1,0:T(8,128)(2,1)}), bf16[2,32,3072]{2,1,0:T(8,128)(2,1)S(1)}, u32[]{:S(2)}, u32[]{:S(2)}) async-start(bf16[2,32,3072]{2,1,0:T(8,128)(2,1)} %bitcast.6), calls=%async_computation.3 | async-start | bytes 786432 | tf_op jit(solution)/shard_map/all_to_all | solution.py:138
